TPU v7x, 256 devices: a whole 4x4x8 slice. The times are simulated.
256 devices in a mesh: seq: 32 (over z, y_hi, core), tp: 8 (over x, y_lo).
Axes of the slice: x: 4, y: 4 (y_hi: 2, y_lo: 2; y = y_hi * 2 + y_lo), z: 8, core: 2. Of those that a mesh axis runs over, the one named last changes fastest.
Arguments:
- stream: bfloat16 [8192, 2048], P('seq', 'tp'), may hold values from -16 to 16
- frames: int32 [8192], P('seq'), may hold values from 0 to 63, never falling along the last dimension, each value on 1 to 256 neighbouring positions
- fidelity: int32 [8192, 1], P('seq'), may hold values from 0 to 15; in each aligned block of 256 rows (0 to 255, 256 to 511, ...) at most 32 rows name the same one
- w_query: bfloat16 [2048, 2048], P(None, 'tp'), may hold values from -2 to 2
- w_key: bfloat16 [2048, 2048], P(None, 'tp'), may hold values from -2 to 2
- w_value: bfloat16 [2048, 2048], P(None, 'tp'), may hold values from -0.125 to 0.125
- w_output: bfloat16 [2048, 2048], P('tp'), may hold values from -0.125 to 0.125
- norm_gain: float32 [2048], replicated, may hold values from 0.1 to 1.9
- expert_gate: bfloat16 [32, 2048, 2816], P('seq', None, 'tp'), may hold values from -0.125 to 0.125
- expert_up: bfloat16 [32, 2048, 2816], P('seq', None, 'tp'), may hold values from -0.125 to 0.125
- expert_down: bfloat16 [32, 2816, 2048], P('seq', 'tp'), may hold values from -0.078125 to 0.078125
Outputs:
- result: bfloat16 [8192, 2048], P('seq', 'tp')
Inputs may be any that keep to these rules, and one draw needn't show every extreme that they name: `frames`: frame numbers never fall along the tokens; a frame holds 1 to 256 tokens, one exactly 256. `fidelity`: among the tokens of one index of seq (aligned blocks of 256 rows) no expert is named more than 32 times, a bound that some block reaches; every expert is named by some token.
All inputs are finite; a program needn't handle non-finite values.
Results may differ from a plain program's by a relative error of at most 0.02.
Values may be sent and summed in bfloat16 or wider, within the bound.
No kernel may reach another device: no remote copies, remote signals or barrier semaphores. Data moves between devices by JAX's collectives and lax.ppermute only.
A program may use at most 128 MiB of HBM per device.

v0:
```python
import math
import jax
import jax.numpy as jnp
from jax import lax
from jax.sharding import PartitionSpec as P

HEAD = 128
EXPERTS = 16
CAP = 32
big_negative = -1e30
norm_eps = 1e-05


def slot_rows(route_ids, tok_rows):
    onehot = (route_ids[:, None] == jnp.arange(EXPERTS, dtype=jnp.int32)[None, :]).astype(jnp.int32)
    places = jnp.sum(onehot * (jnp.cumsum(onehot, axis=0) - 1), axis=1)
    flat_slot = route_ids * CAP + places
    owner_table = (
        jnp.full((EXPERTS * CAP,), tok_rows, jnp.int32)
        .at[flat_slot]
        .set(jnp.arange(tok_rows, dtype=jnp.int32))
    )
    return (flat_slot, owner_table)


def shards(
    stream,
    frames,
    fidelity,
    w_query,
    w_key,
    w_value,
    w_output,
    norm_gain,
    expert_gate,
    expert_up,
    expert_down,
):
    tok_rows, slice_width = stream.shape
    tp_count = lax.axis_size("tp")
    seq_count = lax.axis_size("seq")
    width = slice_width * tp_count
    head_cols = w_query.shape[1]
    heads_here = head_cols // HEAD
    replicas = seq_count // EXPERTS
    col_start = lax.axis_index("tp") * slice_width
    gathered_rows = lax.all_gather(stream, "tp", axis=1, tiled=True)
    query_rows = jnp.dot(gathered_rows, w_query, preferred_element_type=jnp.float32).astype(
        jnp.bfloat16
    )
    key_rows = jnp.dot(gathered_rows, w_key, preferred_element_type=jnp.float32).astype(
        jnp.bfloat16
    )
    value_rows = jnp.dot(gathered_rows, w_value, preferred_element_type=jnp.float32).astype(
        jnp.bfloat16
    )
    query_heads = query_rows.reshape(tok_rows, heads_here, HEAD)
    score_scale = 1.0 / math.sqrt(HEAD)
    top_frame = jnp.max(frames)
    initial = (
        jnp.full((heads_here, tok_rows), big_negative, jnp.float32),
        jnp.zeros((heads_here, tok_rows), jnp.float32),
        jnp.zeros((tok_rows, heads_here, HEAD), jnp.float32),
    )
    key_piece = lax.all_gather(key_rows, "seq", axis=0, tiled=True)
    value_piece = lax.all_gather(value_rows, "seq", axis=0, tiled=True)
    frame_piece = lax.all_gather(frames, "seq", axis=0, tiled=True)

    def update(state):
        run_max, run_total, run_acc = state
        key_heads = key_piece.reshape(key_piece.shape[0], heads_here, HEAD)
        value_heads = value_piece.reshape(value_piece.shape[0], heads_here, HEAD)
        scores = (
            jnp.einsum("qhd,khd->hqk", query_heads, key_heads, preferred_element_type=jnp.float32)
            * score_scale
        )
        allowed = frame_piece[None, None, :] <= frames[None, :, None]
        scores = jnp.where(allowed, scores, big_negative)
        new_max = jnp.maximum(run_max, jnp.max(scores, axis=2))
        weights = jnp.where(allowed, jnp.exp(scores - new_max[:, :, None]), 0.0)
        new_total = jnp.sum(weights, axis=2)
        product = jnp.einsum(
            "hqk,khd->qhd",
            weights.astype(jnp.bfloat16),
            value_heads,
            preferred_element_type=jnp.float32,
        )
        return (new_max, new_total, product)

    run_max, run_total, run_acc = lax.cond(
        jnp.min(frame_piece) > top_frame, lambda unchanged: unchanged, update, initial
    )
    attended = (
        (run_acc / jnp.transpose(run_total)[:, :, None])
        .reshape(tok_rows, head_cols)
        .astype(jnp.bfloat16)
    )
    projected = jnp.dot(attended, w_output, preferred_element_type=jnp.float32)
    summed = lax.psum(projected.astype(jnp.bfloat16), "tp").astype(jnp.float32)
    mixed_full = (gathered_rows.astype(jnp.float32) + summed).astype(jnp.bfloat16)
    mixed_float = mixed_full.astype(jnp.float32)
    normed_full = (
        mixed_float
        * lax.rsqrt(jnp.mean(mixed_float * mixed_float, axis=1, keepdims=True) + norm_eps)
        * norm_gain[None, :]
    ).astype(jnp.bfloat16)
    mixed_rows = lax.dynamic_slice_in_dim(mixed_full, col_start, slice_width, 1)
    route_ids = fidelity[:, 0]
    flat_slot, owner_table = slot_rows(route_ids, tok_rows)
    padded = jnp.concatenate(
        [normed_full, jnp.zeros((1, normed_full.shape[1]), jnp.bfloat16)], axis=0
    )
    per_expert = jnp.take(padded, owner_table, axis=0).reshape(EXPERTS, CAP, normed_full.shape[1])
    sending = jnp.repeat(per_expert, replicas, axis=0)
    arrived = lax.all_to_all(sending, "seq", split_axis=0, concat_axis=0, tiled=True)
    flat_rows = arrived.reshape(-1, width)
    gate_act = jnp.dot(flat_rows, expert_gate[0], preferred_element_type=jnp.float32)
    up_act = jnp.dot(flat_rows, expert_up[0], preferred_element_type=jnp.float32)
    hidden = (jax.nn.silu(gate_act) * up_act).astype(jnp.bfloat16)
    lowered = jnp.dot(hidden, expert_down[0], preferred_element_type=jnp.float32).reshape(
        arrived.shape[0], arrived.shape[1], width
    )
    results = lax.psum(lowered.astype(jnp.bfloat16), "tp")
    returned = lax.all_to_all(results, "seq", split_axis=0, concat_axis=0, tiled=True)
    out_width = returned.shape[2]
    combined = jnp.sum(
        returned.astype(jnp.float32).reshape(EXPERTS, replicas, CAP, out_width), axis=1
    ).reshape(EXPERTS * CAP, out_width)
    own_rows = jnp.take(combined, flat_slot, axis=0)
    own_rows = lax.dynamic_slice_in_dim(own_rows, col_start, slice_width, 1)
    return (mixed_rows.astype(jnp.float32) + own_rows).astype(jnp.bfloat16)


def solution(mesh):
    return jax.shard_map(
        shards,
        mesh=mesh,
        in_specs=(
            P("seq", "tp"),
            P("seq"),
            P("seq", None),
            P(None, "tp"),
            P(None, "tp"),
            P(None, "tp"),
            P("tp", None),
            P(),
            P("seq", None, "tp"),
            P("seq", None, "tp"),
            P("seq", "tp", None),
        ),
        out_specs=P("seq", "tp"),
        check_vma=False,
    )
```

profile of v0, /device:TPU:4, one launch (start us, length us, event | category | flops | bytes accessed | tf_op | source)
XLA Modules:
  0.0 785.2 jit_solution(12655478996595157357)
XLA Ops:
  7.3 47.9 %all-gather.5.cloned.1.call-done = bf16[256,2048]{1,0:T(8,128)(2,1)} async-done(((bf16[256,256]{1,0:T(8,128)(2,1)}), bf16[256,2048]{1,0:T(8,128)(2,1)}) %all-gather.5.cloned.1.call-update) | async-done | bytes 1048592 | tf_op jit(solution)/shard_map/all_gather | solution.py:47
  55.2 2.7 convolution_convert_fusion.3
  58.0 2.6 convolution_convert_fusion.2
  61.4 44.6 %all-gather = s32[32,1,256]{2,1,0:T(1,128)} all-gather(s32[1,1,256]{2,1,0:T(1,128)S(1)} %bitcast.91), channel_id=1, replica_groups=mesh['seq'=32,'tp'=8] {'seq'}, dimensions={0}, use_global_device_ids=true | all-gather | bytes 33792 | tf_op jit(solution)/shard_map/all_gather | solution.py:67
  106.0 1.5 reduce_min.9
  108.8 1.1 convolution_convert_fusion.4
  109.9 38.8 %all-gather.7.cloned.1.call-done = bf16[8192,256]{1,0:T(8,128)(2,1)} async-done(((bf16[256,256]{1,0:T(8,128)(2,1)}), bf16[8192,256]{1,0:T(8,128)(2,1)}) %all-gather.7.cloned.1.call-update) | async-done | bytes 4194320 | tf_op jit(solution)/shard_map/all_gather | solution.py:65
  148.6 86.3 %all-gather.9.cloned.1.call-done = bf16[8192,256]{1,0:T(8,128)(2,1)} async-done(((bf16[256,256]{1,0:T(8,128)(2,1)}), bf16[8192,256]{1,0:T(8,128)(2,1)}) %all-gather.9.cloned.1.call-update) | async-done | bytes 4194320 | tf_op jit(solution)/shard_map/all_gather | solution.py:66
  234.9 36.7 %conditional.1 = (f32[2,256]{1,0:T(2,128)S(1)}, f32[256,2,128]{0,2,1:T(8,128)}) conditional(s32[]{:T(128)} %convert_element_type.58, (s32[8192]{0:T(1024)}, s32[256]{0:T(256)S(1)}, bf16[256,256]{1,0:T(8,128)(2,1)}, bf16[8192,256]{1,0:T(8,128)(2,1)}, bf16[8192,256]{1,0:T(8,128)(2,1)}) %tuple.33, () %tuple.14), branch_computations={%region_2.5_spmd, %region_5.6_spmd} | conditional | flops 2204106240 | bytes 143570000 | solution.py:90
  234.9 2.1 broadcast_compare_fusion
  237.0 12.8 %fusion = (f32[2,256]{1,0:T(2,128)S(1)}, f32[2,256,8192]{2,1,0:T(8,128)}) fusion(pred[256,8192]{1,0:T(8,128)(4,1)S(1)} %broadcast_compare_fusion, bf16[8192,256]{1,0:T(8,128)(2,1)} %get-tuple-element.19, bf16[256,256]{1,0:T(8,128)(2,1)} %get-tuple-element.18), kind=kOutput, calls=%fused_computation.5 | convolution fusion | flops 1086324224 | bytes 23201792 | tf_op jit(solution)/shard_map/cond/branch_0_fun/qhd,khd->hqk/dot_general | solution.py:74
  249.8 9.2 %fusion.2 = f32[2,256]{1,0:T(2,128)S(1)} fusion(f32[2,256,8192]{2,1,0:T(8,128)} %get-tuple-element.31, f32[2,256]{1,0:T(2,128)S(1)} %broadcast_maximum_fusion, pred[256,8192]{1,0:T(8,128)(4,1)} %copy-done.3), kind=kLoop, calls=%fused_computation.7 | loop fusion | flops 20971008 | bytes 18878464 | tf_op jit(solution)/shard_map/cond/branch_0_fun/reduce_sum | solution.py:81
  259.0 2.1 copy-done.1
  261.1 8.8 %fusion.11 = f32[256,2,128]{2,0,1:T(8,128)} fusion(f32[2,256,8192]{2,1,0:T(8,128)S(1)} %copy-done.1, f32[2,256]{1,0:T(2,128)S(1)} %broadcast_maximum_fusion, pred[256,8192]{1,0:T(8,128)(4,1)} %copy-done.3, bf16[8192,256]{1,0:T(8,128)(2,1)} %get-tuple-element.20), kind=kOutput, calls=%fused_computation.16 | convolution fusion | flops 1094713344 | bytes 23332864 | tf_op jit(solution)/shard_map/cond/branch_0_fun/hqk,khd->qhd/dot_general | solution.py:82
  269.9 1.8 copy.28
  272.7 1.5 convolution_convert_fusion.1
  275.7 1.4 scatter_custom_fusion
  277.2 75.0 %all-reduce.4.cloned.1.call-done = bf16[256,2048]{1,0:T(8,128)(2,1)} async-done(((bf16[256,2048]{1,0:T(8,128)(2,1)}), bf16[256,2048]{1,0:T(8,128)(2,1)}) %all-reduce.4.cloned.1.call-update) | async-done | bytes 1048592 | tf_op jit(solution)/shard_map/psum | solution.py:99
  352.2 1.7 fusion.21
  353.9 1.1 copy-done.4
  355.4 3.3 gather_fusion
  358.7 1.8 broadcast_select_fusion
  361.2 105.9 %all_to_all.10 = bf16[32,32,2048]{2,1,0:T(8,128)(2,1)S(1)} all-to-all(bf16[32,32,2048]{2,1,0:T(8,128)(2,1)S(1)} %bitcast.84), channel_id=1, replica_groups=mesh['seq'=32,'tp'=8] {'seq'}, dimensions={0} | all-to-all | bytes 8388608 | tf_op jit(solution)/shard_map/all_to_all | solution.py:115
  467.1 1.7 fusion.26
  468.8 1.8 fusion.28
  471.0 4.3 convolution_convert_fusion
  475.3 185.1 %all-reduce.6.cloned.1.call-done = bf16[32,32,2048]{2,1,0:T(8,128)(2,1)} async-done(((bf16[32,32,2048]{2,1,0:T(8,128)(2,1)}), bf16[32,32,2048]{2,1,0:T(8,128)(2,1)}) %all-reduce.6.cloned.1.call-update) | async-done | bytes 4194320 | tf_op jit(solution)/shard_map/psum | solution.py:123
  660.4 9.9 %all-to-all-start.1 = ((bf16[32,32,2048]{2,1,0:T(8,128)(2,1)}), bf16[32,32,2048]{2,1,0:T(8,128)(2,1)}, u32[]{:S(2)}, u32[]{:S(2)}) async-start(bf16[32,32,2048]{2,1,0:T(8,128)(2,1)} %all-reduce.6.cloned.1.call-done), calls=%async_computation.1 | async-start | bytes 8388608 | tf_op jit(solution)/shard_map/all_to_all | solution.py:124
  670.3 96.5 %all-to-all-done.1 = bf16[32,32,2048]{2,1,0:T(8,128)(2,1)} async-done(((bf16[32,32,2048]{2,1,0:T(8,128)(2,1)}), bf16[32,32,2048]{2,1,0:T(8,128)(2,1)}, u32[]{:S(2)}, u32[]{:S(2)}) %all-to-all-start.1) | async-done | bytes 4194336 | tf_op jit(solution)/shard_map/all_to_all | solution.py:124
  766.8 5.6 convert_reduce_fusion
  772.4 4.6 gather_fusion.1
  777.0 1.7 fusion.32
  (55 shorter events, 5.5 us)
Async XLA Ops:
  6.5 464.5 %copy-start = (bf16[1,352,2048]{2,1,0:T(8,128)(2,1)S(1)}, bf16[1,352,2048]{2,1,0:T(8,128)(2,1)}, u32[]{:S(2)}) copy-start(bf16[1,352,2048]{2,1,0:T(8,128)(2,1)} %param.23) | copy-start | bytes 4325380
  6.5 54.2 %copy-start.7 = (s32[256]{0:T(256)S(1)}, s32[256]{0:T(256)}, u32[]{:S(2)}) copy-start(s32[256]{0:T(256)} %param.14) | copy-start | bytes 3076
  6.5 102.2 %copy-start.5 = (bf16[2048,256]{1,0:T(8,128)(2,1)S(1)}, bf16[2048,256]{1,0:T(8,128)(2,1)}, u32[]{:S(2)}) copy-start(bf16[2048,256]{1,0:T(8,128)(2,1)} %param.16) | copy-start | bytes 3145732
  6.5 48.7 %all-gather.5.cloned.1.call-start = ((), (), s32[]{:S(2)}) async-start(), calls=%async_computation.2 | async-start | bytes 1179648 | tf_op jit(solution)/shard_map/all_gather | solution.py:47
  7.3 141.4 %all-gather.7.cloned.1.call-start = ((), (), s32[]{:S(2)}) async-start(), calls=%async_computation.3 | async-start | bytes 4325376 | tf_op jit(solution)/shard_map/all_gather | solution.py:65
  55.2 53.5 %copy-start.2 = (bf16[256,2048]{1,0:T(8,128)(2,1)S(1)}, bf16[256,2048]{1,0:T(8,128)(2,1)}, u32[]{:S(2)}) copy-start(bf16[256,2048]{1,0:T(8,128)(2,1)} %all-gather.5.cloned.1.call-done) | copy-start | bytes 3145732
  58.0 177.0 %all-gather.9.cloned.1.call-start = ((), (), s32[]{:S(2)}) async-start(), calls=%async_computation.4 | async-start | bytes 4325376 | tf_op jit(solution)/shard_map/all_gather | solution.py:66
  60.7 291.5 %all-reduce.4.cloned.1.call-start = ((), (), s32[]{:S(2)}) async-start(), calls=%async_computation.5 | async-start | bytes 2097152 | tf_op jit(solution)/shard_map/psum | solution.py:99
  234.9 37.7 %copy-start.6 = (bf16[256,2048]{1,0:T(8,128)(2,1)S(1)}, bf16[256,2048]{1,0:T(8,128)(2,1)}, u32[]{:S(2)}) copy-start(bf16[256,2048]{1,0:T(8,128)(2,1)} %param.19) | copy-start | bytes 3145732
  234.9 39.3 %copy-start.8 = (s32[256,1]{0,1:T(1,128)S(1)}, s32[256,1]{0,1:T(1,128)}, u32[]{:S(2)}) copy-start(s32[256,1]{0,1:T(1,128)} %param.15) | copy-start | bytes 3076
  237.0 12.8 %copy-start.3 = (pred[256,8192]{1,0:T(8,128)(4,1)}, pred[256,8192]{1,0:T(8,128)(4,1)S(1)}, u32[]{:S(2)}) copy-start(pred[256,8192]{1,0:T(8,128)(4,1)S(1)} %broadcast_compare_fusion) | copy-start | bytes 6291460 | tf_op jit(solution)/shard_map/cond
  249.8 11.3 %copy-start.1 = (f32[2,256,8192]{2,1,0:T(8,128)S(1)}, f32[2,256,8192]{2,1,0:T(8,128)}, u32[]{:S(2)}) copy-start(f32[2,256,8192]{2,1,0:T(8,128)} %get-tuple-element.31) | copy-start | bytes 50331652 | tf_op jit(solution)/shard_map/cond
  271.7 83.3 %copy-start.9 = (f32[2048]{0:T(1024)S(1)}, f32[2048]{0:T(1024)}, u32[]{:S(2)}) copy-start(f32[2048]{0:T(1024)} %param.20) | copy-start | bytes 24580
  274.2 386.2 %all-reduce.6.cloned.1.call-start = ((), (), s32[]{:S(2)}) async-start(), calls=%async_computation.6 | async-start | bytes 8388608 | tf_op jit(solution)/shard_map/psum | solution.py:123
  353.9 1.1 copy-start.4
  361.1 105.9 %copy-start.11 = (bf16[1,2048,352]{1,2,0:T(8,128)(2,1)S(1)}, bf16[1,2048,352]{1,2,0:T(8,128)(2,1)}, u32[]{:S(2)}) copy-start(bf16[1,2048,352]{1,2,0:T(8,128)(2,1)} %param.21) | copy-start | bytes 4325380
  467.1 1.8 copy-start.12
  660.4 106.4 %all-to-all-start.1 = ((bf16[32,32,2048]{2,1,0:T(8,128)(2,1)}), bf16[32,32,2048]{2,1,0:T(8,128)(2,1)}, u32[]{:S(2)}, u32[]{:S(2)}) async-start(bf16[32,32,2048]{2,1,0:T(8,128)(2,1)} %all-reduce.6.cloned.1.call-done), calls=%async_computation.1 | async-start | bytes 8388608 | tf_op jit(solution)/shard_map/all_to_all | solution.py:124
  772.4 4.6 copy-start.10
Sparse Core Ops, SparseCore 0:
  9.1 46.1 all-gather.4
  58.1 90.4 all-gather.6
  151.4 83.4 all-gather.8
  274.3 77.8 all-reduce.3
  475.4 184.8 all-reduce.5
where the time goes:
time: 786 us; the launch traced here: 785 us
  waiting for transfers between devices  530 us (67%)
  blocking collectives  151 us (19%)
  matrix products  37.3 us (5%)
  other arithmetic  26.8 us (3%)
  local copies, waits for them, and re-layouts  15.5 us (2%)
  between operations  14.6 us (2%)
  starting transfers between devices  10.1 us (1%)
    psum x1, waiting for transfers between devices, shards(): results = lax.psum(lowered.astype(jnp.bfloat16), 'tp')  185 us
    all_to_all x1, blocking collectives, shards(): lax.all_to_all(sending, 'seq', split_axis=0, concat_axis=0, tiled=True)  106 us
    all_to_all x1, waiting for transfers between devices, shards(): lax.all_to_all(results, 'seq', split_axis=0, concat_axis=0, tiled=True)  96.5 us
    all_gather x1, waiting for transfers between devices, shards(): value_piece = lax.all_gather(value_rows, 'seq', axis=0, tiled=True)  86.3 us
    psum x1, waiting for transfers between devices, shards(): summed = lax.psum(projected.astype(jnp.bfloat16), 'tp').astype(jnp.float32)  75 us
    all_gather x1, waiting for transfers between devices, shards(): gathered_rows = lax.all_gather(stream, 'tp', axis=1, tiled=True)  47.9 us
    all_gather x1, blocking collectives, shards(): frame_piece = lax.all_gather(frames, 'seq', axis=0, tiled=True)  44.6 us
    all_gather x1, waiting for transfers between devices, shards(): key_piece = lax.all_gather(key_rows, 'seq', axis=0, tiled=True)  38.8 us
  transfers between devices with their start and end apart: 6, of which 6 were waited for; matrix products, arithmetic and copies ran while one was open for 1% of the time, Pallas kernels for 0%

commit v1 on v0

--- a/solution.py
+++ b/solution.py
@@ -62,8 +62,11 @@
         jnp.zeros((heads_here, tok_rows), jnp.float32),
         jnp.zeros((tok_rows, heads_here, HEAD), jnp.float32),
     )
-    key_piece = lax.all_gather(key_rows, "seq", axis=0, tiled=True)
-    value_piece = lax.all_gather(value_rows, "seq", axis=0, tiled=True)
+    key_piece, value_piece = jnp.split(
+        lax.all_gather(jnp.concatenate([key_rows, value_rows], 1), "seq", tiled=True, axis=0),
+        [key_rows.shape[1]],
+        1,
+    )
     frame_piece = lax.all_gather(frames, "seq", axis=0, tiled=True)
 
     def update(state):

time: 786 us -> 720 us (0.916)
  waiting for transfers between devices: 530 us -> 468 us
    all_gather x2 -> x1, waiting for transfers between devices: 125 us -> 63.2 us  [shards(): lax.all_gather(jnp.concatenate([key_rows, value_rows], 1), 'seq', tiled=T...]
  transfers between devices with their start and end apart: 6 -> 5, of which waited for: 6 -> 5; matrix products, arithmetic and copies ran while one was open for 1% -> 1% of each run, Pallas kernels for 0% -> 0%
where the time goes in v1:
time: 720 us
  waiting for transfers between devices  468 us (65%)
  blocking collectives  151 us (21%)
  matrix products  31.3 us (4%)
  other arithmetic  27.1 us (4%)
  local copies, waits for them, and re-layouts  18.4 us (3%)
  between operations  14.6 us (2%)
  starting transfers between devices  9.81 us (1%)
    psum x1, waiting for transfers between devices, shards(): results = lax.psum(lowered.astype(jnp.bfloat16), 'tp')  185 us
    all_to_all x1, blocking collectives, shards(): lax.all_to_all(sending, 'seq', split_axis=0, concat_axis=0, tiled=True)  106 us
    all_to_all x1, waiting for transfers between devices, shards(): lax.all_to_all(results, 'seq', split_axis=0, concat_axis=0, tiled=True)  96.7 us
    psum x1, waiting for transfers between devices, shards(): summed = lax.psum(projected.astype(jnp.bfloat16), 'tp').astype(jnp.float32)  74.4 us
    all_gather x1, waiting for transfers between devices, shards(): lax.all_gather(jnp.concatenate([key_rows, value_rows], 1), 'seq', tiled=T...  63.2 us
    all_gather x1, waiting for transfers between devices, shards(): gathered_rows = lax.all_gather(stream, 'tp', axis=1, tiled=True)  47.9 us
    all_gather x1, blocking collectives, shards(): frame_piece = lax.all_gather(frames, 'seq', axis=0, tiled=True)  44.6 us
  transfers between devices with their start and end apart: 5, of which 5 were waited for; matrix products, arithmetic and copies ran while one was open for 1% of the time, Pallas kernels for 0%

profile of v1, /device:TPU:4, one launch (start us, length us, event | category | flops | bytes accessed | tf_op | source)
XLA Modules:
  0.0 719.8 jit_solution(13088445047978022656)
XLA Ops:
  7.3 47.9 %all-gather.4.cloned.1.call-done = bf16[256,2048]{1,0:T(8,128)(2,1)} async-done(((bf16[256,256]{1,0:T(8,128)(2,1)}), bf16[256,2048]{1,0:T(8,128)(2,1)}) %all-gather.4.cloned.1.call-update) | async-done | bytes 1048592 | tf_op jit(solution)/shard_map/all_gather | solution.py:47
  55.2 2.1 convolution_convert_fusion.2
  57.4 2.1 convolution_convert_fusion.3
  60.9 44.6 %all-gather = s32[32,1,256]{2,1,0:T(1,128)} all-gather(s32[1,1,256]{2,1,0:T(1,128)S(1)} %bitcast.79), channel_id=1, replica_groups=mesh['seq'=32,'tp'=8] {'seq'}, dimensions={0}, use_global_device_ids=true | all-gather | bytes 33792 | tf_op jit(solution)/shard_map/all_gather | solution.py:70
  105.6 1.5 reduce_min.9
  108.3 1.1 convolution_convert_fusion.4
  109.4 63.2 %all-gather.6.cloned.1.call-done = bf16[8192,512]{0,1:T(8,128)(2,1)} async-done(((bf16[256,512]{0,1:T(8,128)(2,1)}), bf16[8192,512]{0,1:T(8,128)(2,1)}) %all-gather.6.cloned.1.call-update) | async-done | bytes 8388624 | tf_op jit(solution)/shard_map/all_gather | solution.py:66
  172.6 34.1 %conditional.1 = (f32[2,256]{1,0:T(2,128)S(1)}, f32[256,2,128]{0,2,1:T(8,128)}) conditional(s32[]{:T(128)} %convert_element_type.58, (s32[8192]{0:T(1024)}, s32[256]{0:T(256)S(1)}, bf16[256,256]{1,0:T(8,128)(2,1)}, bf16[8192,512]{0,1:T(8,128)(2,1)}) %tuple.33, () %tuple.14), branch_computations={%region_2.5_spmd, %region_5.6_spmd} | conditional | flops 2204106240 | bytes 93762632 | solution.py:93
  172.6 2.1 broadcast_compare_fusion
  174.7 4.8 fusion.32
  179.5 7.9 %fusion = (f32[2,256]{1,0:T(2,128)S(1)}, f32[2,256,8192]{2,1,0:T(8,128)}) fusion(pred[256,8192]{1,0:T(8,128)(4,1)S(1)} %broadcast_compare_fusion, bf16[8192,2,128]{0,2,1:T(8,128)(2,1)S(1)} %bitcast.75, bf16[256,256]{1,0:T(8,128)(2,1)S(1)} %copy-done.6), kind=kOutput, calls=%fused_computation.5 | convolution fusion | flops 1086324224 | bytes 23201792 | tf_op jit(solution)/shard_map/cond/branch_0_fun/qhd,khd->hqk/dot_general | solution.py:77
  187.4 8.7 %fusion.6 = f32[256,2,128]{2,0,1:T(8,128)} fusion(bf16[8192,2,128]{0,2,1:T(8,128)(2,1)S(1)} %bitcast.74, f32[2,256,8192]{2,1,0:T(8,128)} %get-tuple-element.37, f32[2,256]{1,0:T(2,128)S(1)} %broadcast_maximum_fusion, pred[256,8192]{1,0:T(8,128)(4,1)S(1)} %broadcast_compare_fusion), kind=kOutput, calls=%fused_computation.11 | convolution fusion | flops 1094713344 | bytes 23332864 | tf_op jit(solution)/shard_map/cond/branch_0_fun/hqk,khd->qhd/dot_general | solution.py:85
  196.1 1.8 copy.29
  197.9 8.8 %fusion.2 = f32[2,256]{1,0:T(2,128)S(1)} fusion(f32[2,256,8192]{2,1,0:T(8,128)} %get-tuple-element.37, f32[2,256]{1,0:T(2,128)S(1)} %broadcast_maximum_fusion, pred[256,8192]{1,0:T(8,128)(4,1)} %copy-done.2), kind=kLoop, calls=%fused_computation.7 | loop fusion | flops 20971008 | bytes 18878464 | tf_op jit(solution)/shard_map/cond/branch_0_fun/reduce_sum | solution.py:84
  206.8 1.0 divide_convert_fusion
  207.8 1.5 convolution_convert_fusion.1
  210.8 1.6 scatter_custom_fusion
  212.5 74.4 %all-reduce.4.cloned.1.call-done = bf16[256,2048]{1,0:T(8,128)(2,1)} async-done(((bf16[256,2048]{1,0:T(8,128)(2,1)}), bf16[256,2048]{1,0:T(8,128)(2,1)}) %all-reduce.4.cloned.1.call-update) | async-done | bytes 1048592 | tf_op jit(solution)/shard_map/psum | solution.py:102
  286.9 1.7 fusion.15
  288.6 1.1 copy-done.3
  290.1 3.3 gather_fusion
  293.4 1.8 broadcast_select_fusion
  295.8 105.9 %all_to_all.10 = bf16[32,32,2048]{2,1,0:T(8,128)(2,1)S(1)} all-to-all(bf16[32,32,2048]{2,1,0:T(8,128)(2,1)S(1)} %bitcast.70), channel_id=1, replica_groups=mesh['seq'=32,'tp'=8] {'seq'}, dimensions={0} | all-to-all | bytes 8388608 | tf_op jit(solution)/shard_map/all_to_all | solution.py:118
  401.7 1.7 fusion.20
  403.5 1.8 fusion.22
  405.7 4.3 convolution_convert_fusion
  410.0 185.0 %all-reduce.6.cloned.1.call-done = bf16[32,32,2048]{2,1,0:T(8,128)(2,1)} async-done(((bf16[32,32,2048]{2,1,0:T(8,128)(2,1)}), bf16[32,32,2048]{2,1,0:T(8,128)(2,1)}) %all-reduce.6.cloned.1.call-update) | async-done | bytes 4194320 | tf_op jit(solution)/shard_map/psum | solution.py:126
  595.1 9.7 %all-to-all-start.1 = ((bf16[32,32,2048]{2,1,0:T(8,128)(2,1)}), bf16[32,32,2048]{2,1,0:T(8,128)(2,1)}, u32[]{:S(2)}, u32[]{:S(2)}) async-start(bf16[32,32,2048]{2,1,0:T(8,128)(2,1)} %all-reduce.6.cloned.1.call-done), calls=%async_computation.1 | async-start | bytes 8388608 | tf_op jit(solution)/shard_map/all_to_all | solution.py:127
  604.8 96.7 %all-to-all-done.1 = bf16[32,32,2048]{2,1,0:T(8,128)(2,1)} async-done(((bf16[32,32,2048]{2,1,0:T(8,128)(2,1)}), bf16[32,32,2048]{2,1,0:T(8,128)(2,1)}, u32[]{:S(2)}, u32[]{:S(2)}) %all-to-all-start.1) | async-done | bytes 4194336 | tf_op jit(solution)/shard_map/all_to_all | solution.py:127
  701.4 5.6 convert_reduce_fusion
  707.0 4.6 gather_fusion.1
  711.6 1.7 fusion.26
  (54 shorter events, 5.2 us)
Async XLA Ops:
  6.5 399.2 %copy-start = (bf16[1,352,2048]{2,1,0:T(8,128)(2,1)S(1)}, bf16[1,352,2048]{2,1,0:T(8,128)(2,1)}, u32[]{:S(2)}) copy-start(bf16[1,352,2048]{2,1,0:T(8,128)(2,1)} %param.23) | copy-start | bytes 4325380
  6.5 53.7 %copy-start.7 = (s32[256]{0:T(256)S(1)}, s32[256]{0:T(256)}, u32[]{:S(2)}) copy-start(s32[256]{0:T(256)} %param.14) | copy-start | bytes 3076
  6.5 101.8 %copy-start.4 = (bf16[2048,256]{1,0:T(8,128)(2,1)S(1)}, bf16[2048,256]{1,0:T(8,128)(2,1)}, u32[]{:S(2)}) copy-start(bf16[2048,256]{1,0:T(8,128)(2,1)} %param.16) | copy-start | bytes 3145732
  6.5 48.7 %all-gather.4.cloned.1.call-start = ((), (), s32[]{:S(2)}) async-start(), calls=%async_computation.2 | async-start | bytes 1179648 | tf_op jit(solution)/shard_map/all_gather | solution.py:47
  7.3 165.4 %all-gather.6.cloned.1.call-start = ((), (), s32[]{:S(2)}) async-start(), calls=%async_computation.3 | async-start | bytes 8650752 | tf_op jit(solution)/shard_map/all_gather | solution.py:66
  55.2 53.1 %copy-start.1 = (bf16[256,2048]{1,0:T(8,128)(2,1)S(1)}, bf16[256,2048]{1,0:T(8,128)(2,1)}, u32[]{:S(2)}) copy-start(bf16[256,2048]{1,0:T(8,128)(2,1)} %all-gather.4.cloned.1.call-done) | copy-start | bytes 3145732
  60.2 226.6 %all-reduce.4.cloned.1.call-start = ((), (), s32[]{:S(2)}) async-start(), calls=%async_computation.4 | async-start | bytes 2097152 | tf_op jit(solution)/shard_map/psum | solution.py:102
  172.6 35.1 %copy-start.5 = (bf16[256,2048]{1,0:T(8,128)(2,1)S(1)}, bf16[256,2048]{1,0:T(8,128)(2,1)}, u32[]{:S(2)}) copy-start(bf16[256,2048]{1,0:T(8,128)(2,1)} %param.19) | copy-start | bytes 3145732
  172.6 36.7 %copy-start.8 = (s32[256,1]{0,1:T(1,128)S(1)}, s32[256,1]{0,1:T(1,128)}, u32[]{:S(2)}) copy-start(s32[256,1]{0,1:T(1,128)} %param.15) | copy-start | bytes 3076
  174.7 12.7 %copy-start.2 = (pred[256,8192]{1,0:T(8,128)(4,1)}, pred[256,8192]{1,0:T(8,128)(4,1)S(1)}, u32[]{:S(2)}) copy-start(pred[256,8192]{1,0:T(8,128)(4,1)S(1)} %broadcast_compare_fusion) | copy-start | bytes 6291460 | tf_op jit(solution)/shard_map/cond
  174.7 4.8 copy-start.6
  206.8 82.9 %copy-start.9 = (f32[2048]{0:T(1024)S(1)}, f32[2048]{0:T(1024)}, u32[]{:S(2)}) copy-start(f32[2048]{0:T(1024)} %param.20) | copy-start | bytes 24580
  209.3 385.8 %all-reduce.6.cloned.1.call-start = ((), (), s32[]{:S(2)}) async-start(), calls=%async_computation.5 | async-start | bytes 8388608 | tf_op jit(solution)/shard_map/psum | solution.py:126
  288.6 1.1 copy-start.3
  295.8 105.9 %copy-start.11 = (bf16[1,2048,352]{1,2,0:T(8,128)(2,1)S(1)}, bf16[1,2048,352]{1,2,0:T(8,128)(2,1)}, u32[]{:S(2)}) copy-start(bf16[1,2048,352]{1,2,0:T(8,128)(2,1)} %param.21) | copy-start | bytes 4325380
  401.7 1.8 copy-start.12
  595.1 106.4 %all-to-all-start.1 = ((bf16[32,32,2048]{2,1,0:T(8,128)(2,1)}), bf16[32,32,2048]{2,1,0:T(8,128)(2,1)}, u32[]{:S(2)}, u32[]{:S(2)}) async-start(bf16[32,32,2048]{2,1,0:T(8,128)(2,1)} %all-reduce.6.cloned.1.call-done), calls=%async_computation.1 | async-start | bytes 8388608 | tf_op jit(solution)/shard_map/all_to_all | solution.py:127
  707.0 4.6 copy-start.10
Sparse Core Ops, SparseCore 0:
  9.1 46.1 all-gather.3
  60.4 112.2 all-gather.5
  209.4 77.4 all-reduce.3
  410.1 184.8 all-reduce.5
